TPU v7x, 32 devices: a whole 2x2x4 slice. The times are simulated.
32 devices in a mesh: rows: 16 (over z, y, x), cols: 2 (over core).
Axes of the slice: x: 2, y: 2, z: 4, core: 2. Of those that a mesh axis runs over, the one named last changes fastest.
Arguments:
- parent_front: float32 [4096, 2048], P('rows', 'cols')
- right_sides: float32 [4096, 64], P('rows'), may hold values from -6 to 6
- child_values: float32 [1024, 1024], P('rows', 'cols'), may hold values from -6 to 6
- block_owner: int32 [256], P('rows'), may hold values from 0 to 15, as said below
- row_map: int32 [1024], P('rows'), may hold values from 0 to 255
- col_map: int32 [1024], P('cols'), may hold values from 0 to 1023, as said below
Outputs:
- updated: float32 [4096, 2048], P('rows', 'cols')
- side_coeffs: float32 [128, 64], replicated
- side_left: float32 [4096, 64], P('rows')
Inputs may be any that keep to these rules, and one draw needn't show every extreme that they name: `block_owner`: for every k, entries k * 16 to (k + 1) * 16 - 1 form a permutation of 0 to 15. `col_map`: each aligned run of 512 entries is strictly increasing, starts with 0 and ends with 1023.
All inputs are finite; a program needn't handle non-finite values.
Results may differ from a plain program's by a relative error of at most 0.0003.
Values sent between devices are 32-bit elements; how exact they have to be, the bound alone decides.
A program may use at most 64 MiB of HBM per device.

v0:
```python
import jax
import jax.numpy as jnp
from jax import lax
from jax.sharding import PartitionSpec as P

PANEL = 128


highest = lax.Precision.HIGHEST


def spread_2(value, axis, source):
    kept = jnp.where(lax.axis_index(axis) == source, value, 0).astype(value.dtype)
    return lax.psum(kept, axis)


def swapped(block, axis, stride):
    count = lax.axis_size(axis)
    route = []
    for low in range(count):
        high = low | 1 << stride
        if high != low and high < count:
            route += [(low, high), (high, low)]
    return lax.ppermute(block, axis, route)


def matmul(left, right):
    return jnp.dot(left, right, precision=highest, preferred_element_type=jnp.float32)


def lower_inverse(lower):
    order = lower.shape[0]
    if order <= 16:
        return jax.scipy.linalg.solve_triangular(
            lower, jnp.eye(order, dtype=jnp.float32), lower=True
        )
    half = order // 2
    first_inv = lower_inverse(lower[:half, :half])
    second_inv = lower_inverse(lower[half:, half:])
    corner = -matmul(second_inv, matmul(lower[half:, :half], first_inv))
    top = jnp.concatenate([first_inv, jnp.zeros((half, order - half), jnp.float32)], axis=1)
    bottom = jnp.concatenate([corner, second_inv], axis=1)
    return jnp.concatenate([top, bottom], axis=0)


def shards(parent_front, right_sides, child_values, block_owner, row_map, col_map):
    blocks_count = lax.axis_size("rows")
    rows_dev, cols_dev = parent_front.shape
    child_rows, child_cols = child_values.shape
    block_rows = child_rows // blocks_count
    grouped = child_values.reshape(blocks_count, block_rows, child_cols)
    targets = row_map.astype(jnp.float32).reshape(blocks_count, block_rows)
    ordered = jnp.zeros_like(grouped).at[block_owner].set(grouped)
    placed = jnp.zeros_like(targets).at[block_owner].set(targets)
    spread = (
        jnp.zeros((blocks_count, block_rows, cols_dev), jnp.float32).at[:, :, col_map].set(ordered)
    )
    arrived, landing = (
        lax.all_to_all(spread, "rows", split_axis=0, concat_axis=0, tiled=True),
        lax.all_to_all(placed, "rows", split_axis=0, concat_axis=0, tiled=True),
    )
    where_rows = landing.reshape(-1).astype(jnp.int32)
    assembled = parent_front.at[where_rows].add(arrived.reshape(-1, cols_dev))
    panel_rows = spread_2(assembled[:, :PANEL], "cols", 0)
    stacked = jnp.concatenate([assembled, right_sides], axis=1)
    products = matmul(panel_rows.T, stacked)
    gram_matrix = matmul(panel_rows.T, panel_rows)
    lower = jnp.linalg.cholesky(gram_matrix)
    inverse = lower_inverse(lower)
    reduced = matmul(inverse, products)
    upper = lower.T
    levels = blocks_count.bit_length() - 1
    for level in range(levels):
        packed = jnp.concatenate([upper, reduced], axis=1)
        partner = swapped(packed, "rows", level)
        other_upper = partner[:, :PANEL]
        other_reduced = partner[:, PANEL:]
        node_gram = matmul(upper.T, upper) + matmul(other_upper.T, other_upper)
        lower = jnp.linalg.cholesky(node_gram)
        inverse = lower_inverse(lower)
        joined = matmul(upper.T, reduced) + matmul(other_upper.T, other_reduced)
        reduced = matmul(inverse, joined)
        upper = lower.T
    coefs = matmul(inverse.T, reduced)
    remainder = stacked - matmul(panel_rows, coefs)
    updated = remainder[:, :cols_dev]
    side_left = remainder[:, cols_dev:]
    side_coeffs = coefs[:, cols_dev:]
    return (updated, side_coeffs, side_left)


def solution(mesh):
    in_specs = (
        P("rows", "cols"),
        P("rows", None),
        P("rows", "cols"),
        P("rows"),
        P("rows"),
        P("cols"),
    )
    out_specs = (P("rows", "cols"), P(), P("rows", None))
    return jax.shard_map(shards, mesh=mesh, in_specs=in_specs, out_specs=out_specs, check_vma=False)
```

profile of v0, /device:TPU:0, one launch (start us, length us, event | category | flops | bytes accessed | tf_op | source)
XLA Modules:
  0.0 305.9 jit_solution(11291508165823120388)
XLA Ops:
  9.2 8.3 %all-to-all-start = ((f32[16,1,4]{2,1,0:T(1,128)}), f32[16,1,4]{2,1,0:T(1,128)S(1)}, u32[]{:S(2)}, u32[]{:S(2)}) async-start(f32[16,1,4]{2,1,0:T(1,128)} %bitcast.92), calls=%async_computation | async-start | bytes 16384 | tf_op jit(solution)/shard_map/all_to_all | solution.py:60
  19.3 13.6 %scatter_fusion.1 = f32[16,4,1024]{0,1,2:T(4,128)S(1)} fusion(f32[16,4,1024]{0,1,2:T(4,128)S(1)} %broadcast_in_dim.24, s32[512]{0:T(512)S(1)} %compare_select_fusion, f32[512,16,4]{1,2,0:T(4,128)S(1)} %copy.47), kind=kCustom, calls=%fused_computation.2 | custom fusion | bytes 395264 | tf_op jit(solution)/shard_map/scatter | solution.py:56
  32.9 1.4 copy.48
  34.3 7.0 %all-to-all-start.1 = ((f32[16,4,1024]{2,1,0:T(4,128)}), f32[16,4,1024]{2,1,0:T(4,128)S(1)}, u32[]{:S(2)}, u32[]{:S(2)}) async-start(f32[16,4,1024]{2,1,0:T(4,128)} %copy.48), calls=%async_computation.1 | async-start | bytes 524288 | tf_op jit(solution)/shard_map/all_to_all | solution.py:59
  41.6 9.1 %all-to-all-done.1 = f32[16,4,1024]{2,1,0:T(4,128)S(1)} async-done(((f32[16,4,1024]{2,1,0:T(4,128)}), f32[16,4,1024]{2,1,0:T(4,128)S(1)}, u32[]{:S(2)}, u32[]{:S(2)}) %all-to-all-start.1) | async-done | bytes 262176 | tf_op jit(solution)/shard_map/all_to_all | solution.py:59
  50.8 1.7 scatter_fusion.2
  53.5 15.6 %all-reduce.37.cloned.1.call-done = f32[256,128]{1,0:T(8,128)} async-done(((f32[256,128]{1,0:T(8,128)}), f32[256,128]{1,0:T(8,128)}) %all-reduce.37.cloned.1.call-update) | async-done | bytes 131088 | tf_op jit(solution)/shard_map/psum | solution.py:14
  69.2 1.4 fusion.448
  70.7 11.7 %cholesky.89 = f32[128,128]{1,0:T(8,128)S(1)} custom-call(f32[128,128]{1,0:T(8,128)S(1)} %fusion.141), custom_call_target="Cholesky" | custom-call | tf_op jit(solution)/shard_map/jit(cholesky)/cholesky | solution.py:68
  100.7 1.8 collective-permute-start
  103.4 13.6 %collective-permute-done = f32[128,1216]{0,1:T(8,128)S(1)} collective-permute-done((f32[128,1216]{0,1:T(8,128)S(1)}, f32[128,1216]{0,1:T(8,128)S(1)}, u32[]{:S(2)}, u32[]{:S(2)}) %collective-permute-start) | collective-permute-done | bytes 622624 | tf_op jit(solution)/shard_map/ppermute | solution.py:24
  117.4 11.9 %cholesky.100 = f32[128,128]{1,0:T(8,128)S(1)} custom-call(f32[128,128]{1,0:T(8,128)S(1)} %fusion.140), custom_call_target="Cholesky" | custom-call | tf_op jit(solution)/shard_map/jit(cholesky)/cholesky | solution.py:79
  147.1 1.8 collective-permute-start.1
  149.8 12.7 %collective-permute-done.1 = f32[128,1216]{0,1:T(8,128)S(1)} collective-permute-done((f32[128,1216]{0,1:T(8,128)S(1)}, f32[128,1216]{0,1:T(8,128)S(1)}, u32[]{:S(2)}, u32[]{:S(2)}) %collective-permute-start.1) | collective-permute-done | bytes 622624 | tf_op jit(solution)/shard_map/ppermute | solution.py:24
  162.9 11.7 %cholesky.111 = f32[128,128]{1,0:T(8,128)S(1)} custom-call(f32[128,128]{1,0:T(8,128)S(1)} %fusion.139), custom_call_target="Cholesky" | custom-call | tf_op jit(solution)/shard_map/jit(cholesky)/cholesky | solution.py:79
  186.9 1.2 custom-call.63
  192.4 1.8 collective-permute-start.2
  195.1 11.9 %collective-permute-done.2 = f32[128,1216]{0,1:T(8,128)S(1)} collective-permute-done((f32[128,1216]{0,1:T(8,128)S(1)}, f32[128,1216]{0,1:T(8,128)S(1)}, u32[]{:S(2)}, u32[]{:S(2)}) %collective-permute-start.2) | collective-permute-done | bytes 622624 | tf_op jit(solution)/shard_map/ppermute | solution.py:24
  207.3 12.1 %cholesky.122 = f32[128,128]{1,0:T(8,128)S(1)} custom-call(f32[128,128]{1,0:T(8,128)S(1)} %fusion.138), custom_call_target="Cholesky" | custom-call | tf_op jit(solution)/shard_map/jit(cholesky)/cholesky | solution.py:79
  237.2 2.7 collective-permute-start.3
  240.8 24.4 %collective-permute-done.3 = f32[128,1216]{0,1:T(8,128)S(1)} collective-permute-done((f32[128,1216]{0,1:T(8,128)S(1)}, f32[128,1216]{0,1:T(8,128)S(1)}, u32[]{:S(2)}, u32[]{:S(2)}) %collective-permute-start.3) | collective-permute-done | bytes 622624 | tf_op jit(solution)/shard_map/ppermute | solution.py:24
  265.6 11.7 %cholesky.133 = f32[128,128]{1,0:T(8,128)S(1)} custom-call(f32[128,128]{1,0:T(8,128)S(1)} %fusion.137), custom_call_target="Cholesky" | custom-call | tf_op jit(solution)/shard_map/jit(cholesky)/cholesky | solution.py:79
  287.2 1.3 custom-call.77
  297.5 1.3 copy.63
  (276 shorter events, 98.8 us)
Async XLA Ops:
  7.2 10.4 %copy-start.3 = (f32[64,512]{1,0:T(8,128)S(1)}, f32[64,512]{1,0:T(8,128)}, u32[]{:S(2)}) copy-start(f32[64,512]{1,0:T(8,128)} %param.11) | copy-start | bytes 393220
  7.2 0.7 copy-start.5
  7.2 0.7 copy-start.6
  7.2 10.3 %copy-start.4 = (s32[512]{0:T(512)S(1)}, s32[512]{0:T(512)}, u32[]{:S(2)}) copy-start(s32[512]{0:T(512)} %param.14) | copy-start | bytes 6148
  9.2 25.2 %all-to-all-start = ((f32[16,1,4]{2,1,0:T(1,128)}), f32[16,1,4]{2,1,0:T(1,128)S(1)}, u32[]{:S(2)}, u32[]{:S(2)}) async-start(f32[16,1,4]{2,1,0:T(1,128)} %bitcast.92), calls=%async_computation | async-start | bytes 16384 | tf_op jit(solution)/shard_map/all_to_all | solution.py:60
  34.3 16.5 %copy-start = (f32[256,1024]{1,0:T(8,128)S(1)}, f32[256,1024]{1,0:T(8,128)}, u32[]{:S(2)}) copy-start(f32[256,1024]{1,0:T(8,128)} %param.9) | copy-start | bytes 3145732
  34.3 16.4 %all-to-all-start.1 = ((f32[16,4,1024]{2,1,0:T(4,128)}), f32[16,4,1024]{2,1,0:T(4,128)S(1)}, u32[]{:S(2)}, u32[]{:S(2)}) async-start(f32[16,4,1024]{2,1,0:T(4,128)} %copy.48), calls=%async_computation.1 | async-start | bytes 524288 | tf_op jit(solution)/shard_map/all_to_all | solution.py:59
  41.4 27.8 %all-reduce.37.cloned.1.call-start = ((), (), s32[]{:S(2)}) async-start(), calls=%async_computation.2 | async-start | bytes 262144 | tf_op jit(solution)/shard_map/psum | solution.py:14
  53.5 45.4 %copy-start.2 = (f32[256,64]{0,1:T(8,128)S(1)}, f32[256,64]{0,1:T(8,128)}, u32[]{:S(2)}) copy-start(f32[256,64]{0,1:T(8,128)} %param.10) | copy-start | bytes 196612
  69.2 29.7 %copy-start.1 = (f32[256,128]{1,0:T(8,128)S(1)}, f32[256,128]{1,0:T(8,128)}, u32[]{:S(2)}) copy-start(f32[256,128]{1,0:T(8,128)} %all-reduce.37.cloned.1.call-done) | copy-start | bytes 393220
  100.7 16.3 %collective-permute-start = (f32[128,1216]{0,1:T(8,128)S(1)}, f32[128,1216]{0,1:T(8,128)S(1)}, u32[]{:S(2)}, u32[]{:S(2)}) collective-permute-start(f32[128,1216]{0,1:T(8,128)S(1)} %pad_maximum_fusion.2), channel_id=1, source_target_pairs={{0,2},{2,0},{4,6},{6,4},{8,10},{10,8},{12,14},{14,12},{16,18},{18,... | collective-permute-start | bytes 1867784 | tf_op jit(solution)/shard_map/ppermute | solution.py:24
  147.1 15.4 %collective-permute-start.1 = (f32[128,1216]{0,1:T(8,128)S(1)}, f32[128,1216]{0,1:T(8,128)S(1)}, u32[]{:S(2)}, u32[]{:S(2)}) collective-permute-start(f32[128,1216]{0,1:T(8,128)S(1)} %pad_maximum_fusion.3), channel_id=1, source_target_pairs={{0,4},{4,0},{2,6},{6,2},{8,12},{12,8},{10,14},{14,10},{16,20},{20,... | collective-permute-start | bytes 1867784 | tf_op jit(solution)/shard_map/ppermute | solution.py:24
  192.4 14.6 %collective-permute-start.2 = (f32[128,1216]{0,1:T(8,128)S(1)}, f32[128,1216]{0,1:T(8,128)S(1)}, u32[]{:S(2)}, u32[]{:S(2)}) collective-permute-start(f32[128,1216]{0,1:T(8,128)S(1)} %pad_maximum_fusion.4), channel_id=1, source_target_pairs={{0,8},{8,0},{2,10},{10,2},{4,12},{12,4},{6,14},{14,6},{16,24},{24,... | collective-permute-start | bytes 1867784 | tf_op jit(solution)/shard_map/ppermute | solution.py:24
  237.2 28.0 %collective-permute-start.3 = (f32[128,1216]{0,1:T(8,128)S(1)}, f32[128,1216]{0,1:T(8,128)S(1)}, u32[]{:S(2)}, u32[]{:S(2)}) collective-permute-start(f32[128,1216]{0,1:T(8,128)S(1)} %pad_maximum_fusion.5), channel_id=1, source_target_pairs={{0,16},{16,0},{2,18},{18,2},{4,20},{20,4},{6,22},{22,6},{8,24},{24... | collective-permute-start | bytes 1867784 | tf_op jit(solution)/shard_map/ppermute | solution.py:24
Sparse Core Ops, SparseCore 0:
  53.3 15.8 all-reduce.36
where the time goes:
time: 309 us; the launch traced here: 306 us
  other arithmetic  122 us (39%)
  waiting for transfers between devices  87.4 us (28%)
  matrix products  35.3 us (11%)
  starting transfers between devices  23.5 us (8%)
  local copies, waits for them, and re-layouts  22.5 us (7%)
  between operations  15.1 us (5%)
    ppermute x4, waiting for transfers between devices, swapped(): return lax.ppermute(block, axis, route)  62.6 us
    another operation x12, other arithmetic, shards(): lower = jnp.linalg.cholesky(node_gram)  50.1 us
    another operation x45, other arithmetic, lower_inverse(): jax.scipy.linalg.solve_triangular(lower, jnp.eye(order, dtype=jnp.float32...  49.8 us
    dot_general x95, matrix products, matmul(): jnp.dot(left, right, precision=highest, preferred_element_type=jnp.float32)  27 us
    psum x1, waiting for transfers between devices, spread_2(): return lax.psum(kept, axis)  15.6 us
    scatter x2, local copies, waits for them, and re-layouts, shards(): jnp.zeros((blocks_count, block_rows, cols_dev), jnp.float32)  15 us
    another operation x3, other arithmetic, shards(): lower = jnp.linalg.cholesky(gram_matrix)  12.4 us
    all_to_all x1, waiting for transfers between devices, shards(): lax.all_to_all(spread, 'rows', split_axis=0, concat_axis=0, tiled=True)  9.12 us
  transfers between devices with their start and end apart: 7, of which 6 were waited for; matrix products, arithmetic and copies ran while one was open for 7% of the time, Pallas kernels for 0%

commit v1 on v0

v1 whole, which is shorter than its diff:
```python
import functools

import jax
import jax.numpy as jnp
from jax import lax
from jax.experimental import pallas as pl
from jax.experimental.pallas import tpu as pltpu
from jax.sharding import PartitionSpec as P

PANEL = 128
LANES = 128
SUBLANES = 8
MESH = pl.DeviceIdType.MESH
f32 = jnp.float32
bf16 = jnp.bfloat16


def pieces(value):
    first = value.astype(bf16)
    rest = value - first.astype(f32)
    second = rest.astype(bf16)
    third = (rest - second.astype(f32)).astype(bf16)
    return first, second, third


def dot(left, right, dims, precision=None):
    return lax.dot_general(left, right, (dims, ((), ())), precision=precision, preferred_element_type=f32)


def dot_full(left, right, dims=((1,), (0,))):
    return dot(left, right, dims, lax.Precision.HIGHEST)


def sweep_pair(mat, k, lane, sub):
    row0, row1 = mat[k : k + 1, :], mat[k + 1 : k + 2, :]
    col0, col1 = mat[:, k : k + 1], mat[:, k + 1 : k + 2]
    a, b, d = mat[k : k + 1, k : k + 1], mat[k : k + 1, k + 1 : k + 2], mat[k + 1 : k + 2, k + 1 : k + 2]
    ia = 1.0 / a
    ratio = b * ia
    i11 = 1.0 / (d - b * ratio)
    i01 = -ratio * i11
    i00 = ia - ratio * i01
    top0, top1 = i00 * row0 + i01 * row1, i01 * row0 + i11 * row1
    side0, side1 = i00 * col0 + i01 * col1, i01 * col0 + i11 * col1
    lane_row = lane[:1]
    top0 = jnp.where(lane_row == k, -i00, jnp.where(lane_row == k + 1, -i01, top0))
    top1 = jnp.where(lane_row == k, -i01, jnp.where(lane_row == k + 1, -i11, top1))
    raw0 = i00 * row0 + i01 * row1
    raw1 = i01 * row0 + i11 * row1
    out = mat - col0 * raw0 - col1 * raw1
    out = jnp.where(lane == k, side0, jnp.where(lane == k + 1, side1, out))
    out = jnp.where(sub == k, top0, jnp.where(sub == k + 1, top1, out))
    return out


def inverse_of(gram):
    size = gram.shape[0]
    lane = lax.broadcasted_iota(jnp.int32, gram.shape, 1)
    sub = lax.broadcasted_iota(jnp.int32, gram.shape, 0)

    def group(_, mat):
        for k in range(0, SUBLANES, 2):
            mat = sweep_pair(mat, k, lane, sub)
        mat = jnp.concatenate([mat[SUBLANES:], mat[:SUBLANES]], axis=0)
        return pltpu.roll(mat, size - SUBLANES, 1)

    return -lax.fori_loop(0, size // SUBLANES, group, gram)


def kernel(n, ncols, owner, parent, rhs, child, row_map, col_map, updated, side_coeffs, side_left,
           front, send, recv, flat, hot, panel, prod, total, halves, in_sem, a2a_send, a2a_recv, pan_send, pan_recv,
           red_send, red_recv):
    row, col = lax.axis_index("rows"), lax.axis_index("cols")
    rows_dev, cols_dev = front.shape
    child_rows, child_cols = child.shape
    block = child_rows // n
    levels = n.bit_length() - 1
    load = pltpu.make_async_copy(parent, front, in_sem)
    load.start()

    barrier = pltpu.get_barrier_semaphore()
    for step in range(1, n):
        pl.semaphore_signal(barrier, inc=1, device_id=(lax.rem(row + step, n), col), device_id_type=MESH)
    for step in range(1, ncols):
        pl.semaphore_signal(barrier, inc=1, device_id=(row, lax.rem(col + step, ncols)), device_id_type=MESH)

    source = lax.broadcasted_iota(jnp.int32, (1, child_rows), 1)
    target = jnp.zeros((1, child_rows), jnp.int32)
    for k in range(n):
        target = jnp.where(source // block == k, owner[k] * block + source % block, target)
    place = lax.broadcasted_iota(jnp.int32, (child_rows, child_rows), 0) == target
    place_f = jnp.where(place, 1.0, 0.0).astype(f32)
    landing = jnp.sum(place_f * row_map[...].astype(f32), axis=1, keepdims=True)
    place_b = place_f.astype(bf16)
    one, two, three = pieces(child[...])
    ordered = dot(place_b, one, ((1,), (0,))) + dot(place_b, two, ((1,), (0,))) + dot(place_b, three, ((1,), (0,)))
    landing = jnp.broadcast_to(landing, (child_rows, LANES))
    for k in range(n):
        send[k, :, :child_cols] = ordered[k * block : (k + 1) * block]
        send[k, :, child_cols:] = landing[k * block : (k + 1) * block]

    pl.semaphore_wait(barrier, n - 1 + ncols - 1)

    copies = []
    for step in range(1, n):
        peer = lax.rem(row + step, n)
        copy = pltpu.make_async_remote_copy(
            src_ref=send.at[peer], dst_ref=recv.at[row], send_sem=a2a_send.at[step], recv_sem=a2a_recv.at[step],
            device_id=(peer, col), device_id_type=MESH)
        copy.start()
        copies.append(copy)
    recv[row] = send[row]

    cols_at = lax.broadcasted_iota(jnp.int32, hot.shape, 0)
    hot[...] = jnp.where(cols_at == col_map[...], 1.0, 0.0).astype(f32).astype(bf16)
    rhs_pad = prod.shape[1] - cols_dev - PANEL
    load.wait()
    for copy in copies:
        copy.wait()

    for k in range(n):
        flat[k * block : (k + 1) * block, :] = recv[k]
    vals = jnp.concatenate(pieces(flat[:, :child_cols]), axis=0)
    spread3 = dot(vals, hot[...], ((1,), (1,)))
    spread = spread3[:child_rows] + spread3[child_rows : 2 * child_rows] + spread3[2 * child_rows :]
    where_rows = flat[:, child_cols:].astype(jnp.int32)
    rows_at = lax.broadcasted_iota(jnp.int32, where_rows.shape, 1)
    landed = jnp.concatenate(
        [jnp.where(where_rows == rows_at + t * LANES, 1.0, 0.0).astype(f32) for t in range(rows_dev // LANES)], axis=1)
    landed3 = jnp.concatenate([landed] * 3, axis=0).astype(bf16)
    stacked = jnp.concatenate(pieces(spread), axis=0)
    front[...] = front[...] + dot(landed3, stacked, ((0,), (0,)))

    pan_copies = [
        pltpu.make_async_remote_copy(
            src_ref=front.at[:, pl.ds(0, PANEL)], dst_ref=panel, send_sem=pan_send.at[step - 1], recv_sem=pan_recv,
            device_id=(row, step), device_id_type=MESH)
        for step in range(1, ncols)
    ]

    @pl.when(col == 0)
    def _():
        for copy in pan_copies:
            copy.start()
        panel[...] = front[:, :PANEL]
        for copy in pan_copies:
            copy.wait_send()

    @pl.when(col != 0)
    def _():
        pan_copies[0].wait_recv()

    block_panel = panel[...]
    trans = ((0,), (0,))
    prod[:, :cols_dev] = dot_full(block_panel, front[...], trans)
    prod[:, cols_dev : cols_dev + PANEL] = dot_full(block_panel, block_panel, trans)
    sides = jnp.concatenate([rhs[...], jnp.zeros((rows_dev, rhs_pad - rhs.shape[1]), f32)], axis=1)
    prod[:, cols_dev + PANEL :] = dot_full(block_panel, sides, trans)

    tiles = prod.shape[1] // LANES
    nparts = halves.shape[0]
    starts = [tiles * q // nparts * LANES for q in range(nparts + 1)]
    halving = min(levels, (PANEL // SUBLANES).bit_length() - 1)
    lead = min(nparts, levels)
    orders = [[(q + t) % lead for t in range(lead)] + list(range(lead, levels)) for q in range(nparts)]
    base = [jnp.int32(0)] * nparts
    history = [[] for _ in range(nparts)]
    for level in range(levels):
        size = PANEL >> min(level, halving)
        half = size // 2 if level < halving else size
        stage = []
        for q in range(nparts):
            bit = orders[q][level]
            own = (row // (1 << bit)) % 2
            peer = row + (1 - 2 * own) * (1 << bit)
            history[q].append((base[q], own, peer))
            if level < halving:
                keep, give = base[q] + own * half, base[q] + (1 - own) * half
            else:
                keep = give = base[q]
            keep, give = pl.multiple_of(keep, SUBLANES), pl.multiple_of(give, SUBLANES)
            width = starts[q + 1] - starts[q]
            at = sum(
                (PANEL >> (t + 1)) if t < halving else SUBLANES for t in range(level))
            landing_ref = halves.at[q, pl.ds(at, half), pl.ds(0, width)]
            copy = pltpu.make_async_remote_copy(
                src_ref=prod.at[pl.ds(give, half), pl.ds(starts[q], width)], dst_ref=landing_ref,
                send_sem=red_send.at[q, level], recv_sem=red_recv.at[q, level],
                device_id=(peer, col), device_id_type=MESH)
            copy.start()
            stage.append((copy, keep, at, width))
            base[q] = keep
        for q, (copy, keep, at, width) in enumerate(stage):
            copy.wait()
            spot = (pl.ds(keep, half), slice(starts[q], starts[q + 1]))
            prod[spot] = prod[spot] + halves[q, at : at + half, :width]
    size = PANEL >> halving
    for q in range(nparts):
        spot = (pl.ds(base[q], size), slice(starts[q], starts[q + 1]))
        total[spot] = prod[spot]
    for level in reversed(range(halving)):
        size = PANEL >> (level + 1)
        stage = []
        for q in range(nparts):
            older, own, peer = history[q][level]
            keep = pl.multiple_of(older + own * size, SUBLANES)
            spot = total.at[pl.ds(keep, size), pl.ds(starts[q], starts[q + 1] - starts[q])]
            copy = pltpu.make_async_remote_copy(
                src_ref=spot, dst_ref=spot,
                send_sem=red_send.at[q, levels + level], recv_sem=red_recv.at[q, levels + level],
                device_id=(peer, col), device_id_type=MESH)
            copy.start()
            stage.append(copy)
        for copy in stage:
            copy.wait()

    inverse = inverse_of(total[:, cols_dev : cols_dev + PANEL])
    side = dot_full(inverse, total[:, cols_dev + PANEL :])
    coefs = dot_full(inverse, total[:, :cols_dev])
    nrhs = rhs.shape[1]
    side_coeffs[...] = side[:, :nrhs]
    side_left[...] = rhs[...] - dot_full(panel[...], side)[:, :nrhs]
    updated[...] = front[...] - dot_full(panel[...], coefs)


def solution(mesh):
    n, ncols = mesh.shape["rows"], mesh.shape["cols"]

    def shards(parent_front, right_sides, child_values, block_owner, row_map, col_map):
        rows_dev, cols_dev = parent_front.shape
        child_rows, child_cols = child_values.shape
        nrhs = right_sides.shape[1]
        width = cols_dev + PANEL + -(-nrhs // LANES) * LANES
        levels = n.bit_length() - 1
        halving = min(levels, (PANEL // SUBLANES).bit_length() - 1)
        nparts = min(3, levels)
        tiles = width // LANES
        widest = max(tiles * (q + 1) // nparts - tiles * q // nparts for q in range(nparts)) * LANES
        landing_rows = sum((PANEL >> (t + 1)) if t < halving else SUBLANES for t in range(levels))
        block = child_rows // n
        vmem, anywhere = pl.BlockSpec(memory_space=pltpu.VMEM), pl.BlockSpec(memory_space=pl.ANY)
        return pl.pallas_call(
            functools.partial(kernel, n, ncols),
            out_shape=(
                jax.ShapeDtypeStruct((rows_dev, cols_dev), f32),
                jax.ShapeDtypeStruct((PANEL, nrhs), f32),
                jax.ShapeDtypeStruct((rows_dev, nrhs), f32),
            ),
            in_specs=[pl.BlockSpec(memory_space=pltpu.SMEM), anywhere, vmem, vmem, vmem, vmem],
            out_specs=(vmem, vmem, vmem),
            scratch_shapes=[
                pltpu.VMEM((rows_dev, cols_dev), f32),
                pltpu.VMEM((n, block, child_cols + LANES), f32),
                pltpu.VMEM((n, block, child_cols + LANES), f32),
                pltpu.VMEM((child_rows, child_cols + LANES), f32),
                pltpu.VMEM((cols_dev, child_cols), bf16),
                pltpu.VMEM((rows_dev, PANEL), f32),
                pltpu.VMEM((PANEL, width), f32),
                pltpu.VMEM((PANEL, width), f32),
                pltpu.VMEM((nparts, landing_rows, widest), f32),
                pltpu.SemaphoreType.DMA,
                pltpu.SemaphoreType.DMA((n,)),
                pltpu.SemaphoreType.DMA((n,)),
                pltpu.SemaphoreType.DMA((max(ncols - 1, 1),)),
                pltpu.SemaphoreType.DMA,
                pltpu.SemaphoreType.DMA((nparts, 2 * levels)),
                pltpu.SemaphoreType.DMA((nparts, 2 * levels)),
            ],
            compiler_params=pltpu.CompilerParams(collective_id=0, has_side_effects=True, vmem_limit_bytes=48 << 20),
        )(block_owner, parent_front, right_sides, child_values, row_map.reshape(1, -1), col_map.reshape(1, -1))

    in_specs = (
        P("rows", "cols"),
        P("rows", None),
        P("rows", "cols"),
        P("rows"),
        P("rows"),
        P("cols"),
    )
    out_specs = (P("rows", "cols"), P(), P("rows", None))
    return jax.shard_map(shards, mesh=mesh, in_specs=in_specs, out_specs=out_specs, check_vma=False)
```

time: 309 us -> 68.4 us (0.22)
  other arithmetic: 122 us -> 0 us
  waiting for transfers between devices: 87.4 us -> 0 us
  Pallas kernels: 0 us -> 62.9 us
  matrix products: 35.3 us -> 0 us
  starting transfers between devices: 23.5 us -> 0 us
  local copies, waits for them, and re-layouts: 22.5 us -> 4.62 us
  between operations: 15.1 us -> 0.72 us
    another operation x60 -> x0, other arithmetic: 112 us -> none  [the longest x12 50.1 us: shards(): lower = jnp.linalg.cholesky(node_gram)]
    pallas_call x0 -> x1, Pallas kernels: none -> 62.9 us  [shards(): pl.pallas_call(functools.partial(kernel, n, ncols), out_shape=(jax.ShapeD...]
    ppermute x4 -> x0, waiting for transfers between devices: 62.6 us -> none  [swapped(): return lax.ppermute(block, axis, route)]
    dot_general x95 -> x0, matrix products: 27 us -> none  [matmul(): jnp.dot(left, right, precision=highest, preferred_element_type=jnp.float32)]
    scatter x5 -> x0, local copies, waits for them, and re-layouts: 17.6 us -> none  [the longest x2 15 us: shards(): jnp.zeros((blocks_count, block_rows, cols_dev), jnp.float32)]
    psum x1 -> x0, waiting for transfers between devices: 15.6 us -> none  [spread_2(): return lax.psum(kept, axis)]
    all_to_all x2 -> x0, starting transfers between devices: 15.4 us -> none  [the longest x1 8.34 us: shards(): lax.all_to_all(placed, 'rows', split_axis=0, concat_axis=0, tiled=True)]
    all_to_all x2 -> x0, waiting for transfers between devices: 9.12 us -> none  [the longest x1 9.12 us: shards(): lax.all_to_all(spread, 'rows', split_axis=0, concat_axis=0, tiled=True)]
  transfers between devices with their start and end apart: 7 -> 0, of which waited for: 6 -> 0; matrix products, arithmetic and copies ran while one was open for 7% -> 0% of each run, Pallas kernels for 0% -> 0%
where the time goes in v1:
time: 68.4 us; the launch traced here: 68.3 us
  Pallas kernels  62.9 us (92%)
  local copies, waits for them, and re-layouts  4.62 us (7%)
  between operations  0.72 us (1%)
    pallas_call x1, Pallas kernels, shards(): pl.pallas_call(functools.partial(kernel, n, ncols), out_shape=(jax.ShapeD...  62.9 us
    unnamed x12, local copies, waits for them, and re-layouts  3.21 us
    pallas_call x2, local copies, waits for them, and re-layouts, shards(): pl.pallas_call(functools.partial(kernel, n, ncols), out_shape=(jax.ShapeD...  1.41 us

profile of v1, /device:TPU:0, one launch (start us, length us, event | category | flops | bytes accessed | tf_op | source)
XLA Modules:
  0.0 68.3 jit_solution(10002270786465563439)
XLA Ops:
  0.6 0.0 copy-start.1
  0.6 0.0 copy-start.2
  0.7 0.0 copy-start.3
  0.7 0.0 copy-start.4
  0.7 1.0 %copy.9.rhs = f32[256,64]{1,0:T(8,128)S(1)} copy(f32[256,64]{0,1:T(8,128)} %param.7) | data formatting | bytes 131072 | tf_op args[1]
  1.7 0.0 copy-done.1
  1.7 0.0 copy-done.2
  1.7 0.0 copy-done.3
  1.7 0.0 copy-done.4
  1.7 0.0 copy-start
  1.7 1.2 %copy-done = f32[256,1024]{1,0:T(8,128)S(1)} copy-done((f32[256,1024]{1,0:T(8,128)S(1)}, f32[256,1024]{1,0:T(8,128)}, u32[]{:S(2)}) %copy-start) | copy-done | bytes 1048600
  2.9 62.9 %shard_map.85 = (f32[256,1024]{1,0:T(8,128)S(1)}, f32[128,64]{1,0:T(8,128)S(1)}, f32[256,64]{1,0:T(8,128)S(1)}) custom-call(s32[16]{0:T(128)S(1)} %copy-done.3, f32[256,1024]{1,0:T(8,128)S(1)} %copy-done, f32[256,64]{1,0:T(8,128)S(1)} %copy.9.rhs, f32[64,512]{1,0:T(8,128)S(1)} %copy-done.1, s32[1,64]{1,0:T(1,128)S(1)} %bitcast.3, s32[1,512]{1,0:T(1,128)S(1)} %bitcast.2), custom_call_target="tpu_custom_call" | custom-call | tf_op jit(solution)/shard_map/pallas_call | solution.py:242
  65.9 0.7 %copy.10 = f32[128,64]{0,1:T(8,128)} copy(f32[128,64]{1,0:T(8,128)S(1)} %get-tuple-element.4) | data formatting | bytes 65536 | tf_op jit(solution)/shard_map/pallas_call | solution.py:242
  66.6 0.7 %copy.11 = f32[256,64]{0,1:T(8,128)} copy(f32[256,64]{1,0:T(8,128)S(1)} %get-tuple-element.5) | data formatting | bytes 131072 | tf_op jit(solution)/shard_map/pallas_call | solution.py:242
  67.3 1.0 %copy.13 = f32[256,1024]{1,0:T(8,128)} copy(f32[256,1024]{1,0:T(8,128)S(1)} %get-tuple-element.9) | data formatting | bytes 2097152
Async XLA Ops:
  0.6 1.0 %copy-start.1 = (f32[64,512]{1,0:T(8,128)S(1)}, f32[64,512]{1,0:T(8,128)}, u32[]{:S(2)}) copy-start(f32[64,512]{1,0:T(8,128)} %child.1) | copy-start | bytes 393220
  0.6 1.0 %copy-start.2 = (s32[512]{0:T(512)S(1)}, s32[512]{0:T(512)}, u32[]{:S(2)}) copy-start(s32[512]{0:T(512)} %param.11) | copy-start | bytes 6148
  0.7 1.0 %copy-start.3 = (s32[16]{0:T(128)S(1)}, s32[16]{0:T(128)}, u32[]{:S(2)}) copy-start(s32[16]{0:T(128)} %owner.1) | copy-start | bytes 196
  0.7 1.0 %copy-start.4 = (s32[64]{0:T(128)S(1)}, s32[64]{0:T(128)}, u32[]{:S(2)}) copy-start(s32[64]{0:T(128)} %param.10) | copy-start | bytes 772
  1.7 1.2 %copy-start = (f32[256,1024]{1,0:T(8,128)S(1)}, f32[256,1024]{1,0:T(8,128)}, u32[]{:S(2)}) copy-start(f32[256,1024]{1,0:T(8,128)} %parent.1) | copy-start | bytes 3145732

commit v2 on v1

v2 whole, which is shorter than its diff:
```python
import functools

import jax
import jax.numpy as jnp
from jax import lax
from jax.experimental import pallas as pl
from jax.experimental.pallas import tpu as pltpu
from jax.sharding import PartitionSpec as P

PANEL = 128
LANES = 128
SUBLANES = 8
VMEM_LIMIT = 40 << 20
MESH = pl.DeviceIdType.MESH
f32 = jnp.float32
bf16 = jnp.bfloat16


def pieces(value):
    first = value.astype(bf16)
    rest = value - first.astype(f32)
    second = rest.astype(bf16)
    third = (rest - second.astype(f32)).astype(bf16)
    return first, second, third


def dot(left, right, dims, precision=None):
    return lax.dot_general(left, right, (dims, ((), ())), precision=precision, preferred_element_type=f32)


def dot_full(left, right, dims=((1,), (0,))):
    return dot(left, right, dims, lax.Precision.HIGHEST)


def sweep_pair(mat, k, lane, sub):
    row0, row1 = mat[k : k + 1, :], mat[k + 1 : k + 2, :]
    col0, col1 = mat[:, k : k + 1], mat[:, k + 1 : k + 2]
    a, b, d = mat[k : k + 1, k : k + 1], mat[k : k + 1, k + 1 : k + 2], mat[k + 1 : k + 2, k + 1 : k + 2]
    ia = 1.0 / a
    ratio = b * ia
    i11 = 1.0 / (d - b * ratio)
    i01 = -ratio * i11
    i00 = ia - ratio * i01
    top0, top1 = i00 * row0 + i01 * row1, i01 * row0 + i11 * row1
    side0, side1 = i00 * col0 + i01 * col1, i01 * col0 + i11 * col1
    lane_row = lane[:1]
    top0 = jnp.where(lane_row == k, -i00, jnp.where(lane_row == k + 1, -i01, top0))
    top1 = jnp.where(lane_row == k, -i01, jnp.where(lane_row == k + 1, -i11, top1))
    raw0 = i00 * row0 + i01 * row1
    raw1 = i01 * row0 + i11 * row1
    out = mat - col0 * raw0 - col1 * raw1
    out = jnp.where(lane == k, side0, jnp.where(lane == k + 1, side1, out))
    out = jnp.where(sub == k, top0, jnp.where(sub == k + 1, top1, out))
    return out


def sweep_groups(mat, count):
    size = mat.shape[0]
    lane = lax.broadcasted_iota(jnp.int32, mat.shape, 1)
    sub = lax.broadcasted_iota(jnp.int32, mat.shape, 0)

    def group(_, mat):
        for k in range(0, SUBLANES, 2):
            mat = sweep_pair(mat, k, lane, sub)
        mat = jnp.concatenate([mat[SUBLANES:], mat[:SUBLANES]], axis=0)
        return pltpu.roll(mat, size - SUBLANES, 1)

    return lax.fori_loop(0, count, group, mat)


def plan(n, width):
    levels = n.bit_length() - 1
    halving = min(levels, (PANEL // SUBLANES).bit_length() - 1)
    nparts = min(3, levels)
    tiles = width // LANES
    starts = [tiles * q // nparts * LANES for q in range(nparts + 1)]
    orders = [[(q + t) % nparts for t in range(nparts)] + list(range(nparts, levels)) for q in range(nparts)]
    single = max(halving - 2, 0)
    cuts = [(t, t + 1) for t in range(single)] + [(single, halving)]
    parts = [([order[a:b] for a, b in cuts], [[bit] for bit in order[halving:]]) for order in orders]
    return starts, parts, halving


def slots_of(n):
    levels = n.bit_length() - 1
    halving = min(levels, (PANEL // SUBLANES).bit_length() - 1)
    rows, count = 0, 0
    single = max(halving - 2, 0)
    size = PANEL
    for bits in [1] * single + [halving - single]:
        size >>= bits
        rows += ((1 << bits) - 1) * size
        count += (1 << bits) - 1
    rows += (levels - halving) * SUBLANES
    count += levels - halving
    return rows, count


def kernel(n, ncols, owner, parent, rhs_t, child_hbm, row_map, col_map, front, panel, coefs, side_t, left_t,
           child, send, recv, flat, hot, sides, prod, total, halves, gram, gram_in, gram_all,
           in_sem, a2a_send, a2a_recv, pan_send, pan_recv, gram_send, gram_recv, red_send, red_recv):
    row, col = lax.axis_index("rows"), lax.axis_index("cols")
    rows_dev, cols_dev = front.shape
    child_rows, child_cols = child.shape
    nrhs = rhs_t.shape[0]
    block = child_rows // n
    load_child = pltpu.make_async_copy(child_hbm, child, in_sem.at[0])
    load_child.start()
    load = pltpu.make_async_copy(parent, front, in_sem.at[1])
    load.start()

    barrier = pltpu.get_barrier_semaphore()
    for step in range(1, n):
        pl.semaphore_signal(barrier, inc=1, device_id=(lax.rem(row + step, n), col), device_id_type=MESH)
    for step in range(1, ncols):
        pl.semaphore_signal(barrier, inc=1, device_id=(row, lax.rem(col + step, ncols)), device_id_type=MESH)

    source = lax.broadcasted_iota(jnp.int32, (1, child_rows), 1)
    target = jnp.zeros((1, child_rows), jnp.int32)
    for k in range(n):
        target = jnp.where(source // block == k, owner[k] * block + source % block, target)
    place = lax.broadcasted_iota(jnp.int32, (child_rows, child_rows), 0) == target
    place_f = jnp.where(place, 1.0, 0.0).astype(f32)
    landing = jnp.sum(place_f * row_map[...].astype(f32), axis=1, keepdims=True)
    place_b = place_f.astype(bf16)
    load_child.wait()
    one, two, three = pieces(child[...])
    ordered = dot(place_b, one, ((1,), (0,))) + dot(place_b, two, ((1,), (0,))) + dot(place_b, three, ((1,), (0,)))
    landing = jnp.broadcast_to(landing, (child_rows, LANES))
    for k in range(n):
        send[k, :, :child_cols] = ordered[k * block : (k + 1) * block]
        send[k, :, child_cols:] = landing[k * block : (k + 1) * block]

    pl.semaphore_wait(barrier, n - 1 + ncols - 1)

    copies = []
    for step in range(1, n):
        peer = lax.rem(row + step, n)
        copy = pltpu.make_async_remote_copy(
            src_ref=send.at[peer], dst_ref=recv.at[row], send_sem=a2a_send.at[step], recv_sem=a2a_recv.at[step],
            device_id=(peer, col), device_id_type=MESH)
        copy.start()
        copies.append(copy)
    recv[row] = send[row]

    cols_at = lax.broadcasted_iota(jnp.int32, hot.shape, 0)
    hot[...] = jnp.where(cols_at == col_map[...], 1.0, 0.0).astype(f32).astype(bf16)
    padded = jnp.concatenate([rhs_t[...], jnp.zeros((sides.shape[1] - nrhs, rows_dev), f32)], axis=0)
    sides[...] = jnp.transpose(padded)
    load.wait()
    for copy in copies:
        copy.wait()

    for k in range(n):
        flat[k * block : (k + 1) * block, :] = recv[k]
    vals = jnp.concatenate(pieces(flat[:, :child_cols]), axis=0)
    where_rows = flat[:, child_cols:].astype(jnp.int32)
    rows_at = lax.broadcasted_iota(jnp.int32, where_rows.shape, 1)
    landed = jnp.concatenate(
        [jnp.where(where_rows == rows_at + t * LANES, 1.0, 0.0).astype(f32) for t in range(rows_dev // LANES)], axis=1)
    landed3 = jnp.concatenate([landed] * 3, axis=0).astype(bf16)

    def assemble(first, last):
        spread3 = dot(vals, hot[first:last, :], ((1,), (1,)))
        spread = spread3[:child_rows] + spread3[child_rows : 2 * child_rows] + spread3[2 * child_rows :]
        stacked = jnp.concatenate(pieces(spread), axis=0)
        front[:, first:last] = front[:, first:last] + dot(landed3, stacked, ((0,), (0,)))

    assemble(0, PANEL)
    pan_copies = [
        pltpu.make_async_remote_copy(
            src_ref=front.at[:, pl.ds(0, PANEL)], dst_ref=panel, send_sem=pan_send.at[step - 1], recv_sem=pan_recv,
            device_id=(row, step), device_id_type=MESH)
        for step in range(1, ncols)
    ]

    @pl.when(col == 0)
    def _():
        for copy in pan_copies:
            copy.start()
        panel[...] = front[:, :PANEL]

    assemble(PANEL, cols_dev)

    @pl.when(col == 0)
    def _():
        for copy in pan_copies:
            copy.wait_send()

    @pl.when(col != 0)
    def _():
        pan_copies[0].wait_recv()

    block_panel = panel[...]
    trans = ((0,), (0,))
    gram[...] = dot_full(block_panel, block_panel, trans)

    chunks = min(n, PANEL // SUBLANES)
    chunk = PANEL // chunks
    own_chunk = lax.rem(row, chunks)
    own_rows = pl.ds(pl.multiple_of(own_chunk * chunk, SUBLANES), chunk)
    gathers = []
    for step in range(1, n):
        peer = lax.rem(row + step, n)
        start = pl.multiple_of(lax.rem(peer, chunks) * chunk, SUBLANES)
        copy = pltpu.make_async_remote_copy(
            src_ref=gram.at[pl.ds(start, chunk)], dst_ref=gram_in.at[row],
            send_sem=gram_send.at[step], recv_sem=gram_recv.at[step], device_id=(peer, col), device_id_type=MESH)
        copy.start()
        gathers.append(copy)
    gram_in[row] = gram[own_rows, :]

    prod[:, :cols_dev] = dot_full(block_panel, front[...], trans)
    prod[:, cols_dev:] = dot_full(block_panel, sides[...], trans)

    starts, parts, halving = plan(n, prod.shape[1])
    base = [row * 0] * len(parts)
    nstages = len(parts[0][0])

    def own_bit(bit):
        return (row // (1 << bit)) % 2

    def members(bits):
        mine = sum(own_bit(bit) * (1 << i) for i, bit in enumerate(bits))
        others = []
        for d in range(1, 1 << len(bits)):
            code, peer = 0, row
            for i, bit in enumerate(bits):
                own = own_bit(bit)
                flip = d >> i & 1
                code = code + (1 - own if flip else own) * (1 << i)
                peer = peer + ((1 - 2 * own) * (1 << bit) if flip else 0)
            others.append((code, peer))
        return mine, others

    def send_stage(stage, at, slot, size, split):
        held = []
        for q, (groups, extras) in enumerate(parts):
            bits = groups[stage] if split else extras[stage]
            mine, others = members(bits)
            piece = size >> len(bits) if split else size
            keep = pl.multiple_of(base[q] + mine * piece if split else base[q], SUBLANES)
            width = starts[q + 1] - starts[q]
            sent = []
            for d, (code, peer) in enumerate(others):
                give = pl.multiple_of(base[q] + code * piece, SUBLANES) if split else keep
                copy = pltpu.make_async_remote_copy(
                    src_ref=prod.at[pl.ds(give, piece), pl.ds(starts[q], width)],
                    dst_ref=halves.at[q, pl.ds(at + d * piece, piece), pl.ds(0, width)],
                    send_sem=red_send.at[q, slot + d], recv_sem=red_recv.at[q, slot + d],
                    device_id=(peer, col), device_id_type=MESH)
                copy.start()
                sent.append((copy, at + d * piece))
            held.append((sent, keep, piece, width))
            base[q] = keep
        used = len(held[0][0])
        return held, at + used * held[0][2], slot + used, held[0][2]

    def add_stage(held):
        for q, (sent, keep, piece, width) in enumerate(held):
            for copy, _ in sent:
                copy.wait()
            spot = (pl.ds(keep, piece), slice(starts[q], starts[q + 1]))
            value = prod[spot]
            for _, at in sent:
                value = value + halves[q, at : at + piece, :width]
            prod[spot] = value

    def share_stage(stage, slot, piece):
        sent = []
        for q, (groups, _) in enumerate(parts):
            _, others = members(groups[stage])
            keep = pl.multiple_of(base[q], SUBLANES)
            spot = total.at[pl.ds(keep, piece), pl.ds(starts[q], starts[q + 1] - starts[q])]
            for d, (_, peer) in enumerate(others):
                copy = pltpu.make_async_remote_copy(
                    src_ref=spot, dst_ref=spot, send_sem=red_send.at[q, slot + d], recv_sem=red_recv.at[q, slot + d],
                    device_id=(peer, col), device_id_type=MESH)
                copy.start()
                sent.append(copy)
        return sent, slot + len(sent) // len(parts)

    marks = []
    at, slot, size = 0, 0, PANEL
    marks.append(list(base))
    held, at, slot, size = send_stage(0, at, slot, size, True)

    for copy in gathers:
        copy.wait()
    summed = gram_in[0]
    for k in range(1, n):
        summed = summed + gram_in[k]
    gram_all[own_rows, :] = summed
    spreads = []
    for step in range(1, chunks):
        peer = row - own_chunk + lax.rem(own_chunk + step, chunks)
        copy = pltpu.make_async_remote_copy(
            src_ref=gram_all.at[own_rows], dst_ref=gram_all.at[own_rows],
            send_sem=gram_send.at[n + step], recv_sem=gram_recv.at[n + step],
            device_id=(peer, col), device_id_type=MESH)
        copy.start()
        spreads.append(copy)

    for stage in range(1, nstages):
        add_stage(held)
        marks.append(list(base))
        held, at, slot, size = send_stage(stage, at, slot, size, True)
    for copy in spreads:
        copy.wait()
    turns = PANEL // SUBLANES
    mat, done = gram_all[...], 0

    def turn_by(mat, done, share):
        upto = min(turns, done + share)
        return (sweep_groups(mat, upto - done) if upto > done else mat), upto

    mat, done = turn_by(mat, done, 3)
    add_stage(held)
    for stage in range(len(parts[0][1])):
        held, at, slot, size = send_stage(stage, at, slot, size, False)
        add_stage(held)
    for q in range(len(parts)):
        spot = (pl.ds(pl.multiple_of(base[q], SUBLANES), size), slice(starts[q], starts[q + 1]))
        total[spot] = prod[spot]
    for stage in reversed(range(nstages)):
        sent, slot = share_stage(stage, slot, size)
        mat, done = turn_by(mat, done, turns if stage == 0 else 4)
        for copy in sent:
            copy.wait()
        size <<= len(parts[0][0][stage])
        for q in range(len(parts)):
            base[q] = marks[stage][q]

    inverse = -mat
    side = dot_full(inverse, total[:, cols_dev:])
    coefs[...] = dot_full(inverse, total[:, :cols_dev])
    side_t[...] = jnp.transpose(side)[:nrhs]
    left_t[...] = rhs_t[...] - jnp.transpose(dot_full(panel[...], side))[:nrhs]


def solution(mesh):
    n, ncols = mesh.shape["rows"], mesh.shape["cols"]

    def shards(parent_front, right_sides, child_values, block_owner, row_map, col_map):
        rows_dev, cols_dev = parent_front.shape
        child_rows, child_cols = child_values.shape
        nrhs = right_sides.shape[1]
        side_width = -(-nrhs // LANES) * LANES
        width = cols_dev + side_width
        starts, parts, _ = plan(n, width)
        nparts = len(parts)
        widest = max(starts[q + 1] - starts[q] for q in range(nparts))
        landing_rows, slots = slots_of(n)
        block = child_rows // n
        chunks = min(n, PANEL // SUBLANES)
        vmem, anywhere = pl.BlockSpec(memory_space=pltpu.VMEM), pl.BlockSpec(memory_space=pl.ANY)
        dma = pltpu.SemaphoreType.DMA
        front, panel, coefs, side_t, left_t = pl.pallas_call(
            functools.partial(kernel, n, ncols),
            out_shape=(
                jax.ShapeDtypeStruct((rows_dev, cols_dev), f32),
                jax.ShapeDtypeStruct((rows_dev, PANEL), f32),
                jax.ShapeDtypeStruct((PANEL, cols_dev), f32),
                jax.ShapeDtypeStruct((nrhs, PANEL), f32),
                jax.ShapeDtypeStruct((nrhs, rows_dev), f32),
            ),
            in_specs=[pl.BlockSpec(memory_space=pltpu.SMEM), anywhere, vmem, anywhere, vmem, vmem],
            out_specs=(vmem, vmem, vmem, vmem, vmem),
            scratch_shapes=[
                pltpu.VMEM((child_rows, child_cols), f32),
                pltpu.VMEM((n, block, child_cols + LANES), f32),
                pltpu.VMEM((n, block, child_cols + LANES), f32),
                pltpu.VMEM((child_rows, child_cols + LANES), f32),
                pltpu.VMEM((cols_dev, child_cols), bf16),
                pltpu.VMEM((rows_dev, side_width), f32),
                pltpu.VMEM((PANEL, width), f32),
                pltpu.VMEM((PANEL, width), f32),
                pltpu.VMEM((nparts, landing_rows, widest), f32),
                pltpu.VMEM((PANEL, PANEL), f32),
                pltpu.VMEM((n, PANEL // chunks, PANEL), f32),
                pltpu.VMEM((PANEL, PANEL), f32),
                dma((2,)),
                dma((n,)),
                dma((n,)),
                dma((max(ncols - 1, 1),)),
                dma,
                dma((n + chunks,)),
                dma((n + chunks,)),
                dma((nparts, 2 * slots)),
                dma((nparts, 2 * slots)),
            ],
            compiler_params=pltpu.CompilerParams(collective_id=0, has_side_effects=True, vmem_limit_bytes=VMEM_LIMIT),
        )(block_owner, parent_front, right_sides.T, child_values, row_map.reshape(1, -1), col_map.reshape(1, -1))
        updated = front - jnp.dot(panel, coefs, precision=lax.Precision.HIGHEST, preferred_element_type=f32)
        return updated, side_t.T, left_t.T

    in_specs = (
        P("rows", "cols"),
        P("rows", None),
        P("rows", "cols"),
        P("rows"),
        P("rows"),
        P("cols"),
    )
    out_specs = (P("rows", "cols"), P(), P("rows", None))
    return jax.shard_map(shards, mesh=mesh, in_specs=in_specs, out_specs=out_specs, check_vma=False)
```

time: 68.4 us -> 53.2 us (0.78)
  Pallas kernels: 62.9 us -> 45.4 us
  matrix products: 0 us -> 1.98 us
    pallas_call x1, Pallas kernels: 62.9 us -> 45.4 us  [shards(): pl.pallas_call(functools.partial(kernel, n, ncols), out_shape=(jax.ShapeD...]
    dot_general x0 -> x1, matrix products: none -> 1.98 us  [shards(): jnp.dot(panel, coefs, precision=lax.Precision.HIGHEST, preferred_element_...]
    unnamed x12 -> x14, local copies, waits for them, and re-layouts: 3.21 us -> 4.87 us
    pallas_call x2 -> x0, local copies, waits for them, and re-layouts: 1.41 us -> none  [shards(): pl.pallas_call(functools.partial(kernel, n, ncols), out_shape=(jax.ShapeD...]
where the time goes in v2:
time: 53.2 us; the launch traced here: 53 us
  Pallas kernels  45.4 us (85%)
  local copies, waits for them, and re-layouts  4.87 us (9%)
  matrix products  1.98 us (4%)
  between operations  0.67 us (1%)
    pallas_call x1, Pallas kernels, shards(): pl.pallas_call(functools.partial(kernel, n, ncols), out_shape=(jax.ShapeD...  45.4 us
    unnamed x14, local copies, waits for them, and re-layouts  4.87 us
    dot_general x1, matrix products, shards(): jnp.dot(panel, coefs, precision=lax.Precision.HIGHEST, preferred_element_...  1.98 us

profile of v2, /device:TPU:0, one launch (start us, length us, event | category | flops | bytes accessed | tf_op | source)
XLA Modules:
  0.0 53.0 jit_solution(2535770347412087359)
XLA Ops:
  0.6 0.0 copy-start.3
  0.6 0.0 copy-start.4
  0.7 0.0 copy-start.5
  0.7 0.7 %copy-done.3 = s32[512]{0:T(512)S(1)} copy-done((s32[512]{0:T(512)S(1)}, s32[512]{0:T(512)}, u32[]{:S(2)}) %copy-start.3) | copy-done | bytes 2072
  1.3 0.0 copy-done.4
  1.3 0.0 copy-done.5
  1.3 0.0 copy-start
  1.3 1.2 %copy-done = f32[256,1024]{1,0:T(8,128)S(1)} copy-done((f32[256,1024]{1,0:T(8,128)S(1)}, f32[256,1024]{1,0:T(8,128)}, u32[]{:S(2)}) %copy-start) | copy-done | bytes 1048600
  2.5 0.0 copy-start.1
  2.5 0.9 %copy-done.1 = f32[64,512]{1,0:T(8,128)S(1)} copy-done((f32[64,512]{1,0:T(8,128)S(1)}, f32[64,512]{1,0:T(8,128)}, u32[]{:S(2)}) %copy-start.1) | copy-done | bytes 131096
  3.5 0.0 copy-start.2
  3.5 0.8 %copy-done.2 = f32[256,64]{0,1:T(8,128)S(1)} copy-done((f32[256,64]{0,1:T(8,128)S(1)}, f32[256,64]{0,1:T(8,128)}, u32[]{:S(2)}) %copy-start.2) | copy-done | bytes 65560
  4.3 45.4 %shard_map.85 = (f32[256,1024]{1,0:T(8,128)S(1)}, f32[256,128]{1,0:T(8,128)S(1)}, f32[128,1024]{1,0:T(8,128)S(1)}, f32[64,128]{1,0:T(8,128)S(1)}, f32[64,256]{1,0:T(8,128)S(1)}) custom-call(s32[16]{0:T(128)S(1)} %copy-done.4, f32[256,1024]{1,0:T(8,128)S(1)} %copy-done, f32[64,256]{1,0:T(8,128)S(1)} %bitcast.7, f32[64,512]{1,0:T(8,128)S(1)} %copy-done.1, ...), custom_call_target="tpu_custom_call" | custom-call | tf_op jit(solution)/shard_map/pallas_call | solution.py:358
  49.7 2.0 %convolution_subtract_fusion = f32[256,1024]{1,0:T(8,128)} fusion(f32[256,1024]{1,0:T(8,128)S(1)} %get-tuple-element.8, f32[256,128]{1,0:T(8,128)S(1)} %get-tuple-element.9, f32[128,1024]{1,0:T(8,128)S(1)} %get-tuple-element.10), kind=kOutput, calls=%fused_computation | convolution fusion | flops 402915328 | bytes 2752512 | tf_op jit(solution)/shard_map/dot_general | solution.py:394
  51.7 0.6 %copy.11 = f32[128,64]{0,1:T(8,128)} copy(f32[128,64]{0,1:T(8,128)S(1)} %bitcast.9) | data formatting | bytes 65536
  52.3 0.6 %copy.12 = f32[256,64]{0,1:T(8,128)} copy(f32[256,64]{0,1:T(8,128)S(1)} %bitcast.8) | data formatting | bytes 131072
Async XLA Ops:
  0.6 0.7 %copy-start.3 = (s32[512]{0:T(512)S(1)}, s32[512]{0:T(512)}, u32[]{:S(2)}) copy-start(s32[512]{0:T(512)} %param.11) | copy-start | bytes 6148
  0.6 0.7 %copy-start.4 = (s32[16]{0:T(128)S(1)}, s32[16]{0:T(128)}, u32[]{:S(2)}) copy-start(s32[16]{0:T(128)} %owner.1) | copy-start | bytes 196
  0.7 0.7 %copy-start.5 = (s32[64]{0:T(128)S(1)}, s32[64]{0:T(128)}, u32[]{:S(2)}) copy-start(s32[64]{0:T(128)} %param.10) | copy-start | bytes 772
  1.3 1.2 %copy-start = (f32[256,1024]{1,0:T(8,128)S(1)}, f32[256,1024]{1,0:T(8,128)}, u32[]{:S(2)}) copy-start(f32[256,1024]{1,0:T(8,128)} %parent.1) | copy-start | bytes 3145732
  2.5 0.9 %copy-start.1 = (f32[64,512]{1,0:T(8,128)S(1)}, f32[64,512]{1,0:T(8,128)}, u32[]{:S(2)}) copy-start(f32[64,512]{1,0:T(8,128)} %child_hbm.1) | copy-start | bytes 393220
  3.5 0.8 %copy-start.2 = (f32[256,64]{0,1:T(8,128)S(1)}, f32[256,64]{0,1:T(8,128)}, u32[]{:S(2)}) copy-start(f32[256,64]{0,1:T(8,128)} %param.7) | copy-start | bytes 196612

commit v3 on v2

--- a/solution.py
+++ b/solution.py
@@ -10,6 +10,7 @@
 PANEL = 128
 LANES = 128
 SUBLANES = 8
+TILE = 256
 VMEM_LIMIT = 40 << 20
 MESH = pl.DeviceIdType.MESH
 f32 = jnp.float32
@@ -32,36 +33,54 @@
     return dot(left, right, dims, lax.Precision.HIGHEST)
 
 
-def sweep_pair(mat, k, lane, sub):
-    row0, row1 = mat[k : k + 1, :], mat[k + 1 : k + 2, :]
-    col0, col1 = mat[:, k : k + 1], mat[:, k + 1 : k + 2]
-    a, b, d = mat[k : k + 1, k : k + 1], mat[k : k + 1, k + 1 : k + 2], mat[k + 1 : k + 2, k + 1 : k + 2]
+def inverse_pair(a, b, d):
     ia = 1.0 / a
     ratio = b * ia
     i11 = 1.0 / (d - b * ratio)
     i01 = -ratio * i11
-    i00 = ia - ratio * i01
-    top0, top1 = i00 * row0 + i01 * row1, i01 * row0 + i11 * row1
-    side0, side1 = i00 * col0 + i01 * col1, i01 * col0 + i11 * col1
+    return ia - ratio * i01, i01, i11
+
+
+def sweep_four(mat, k, lane):
+    cols = [mat[:, k + j : k + j + 1] for j in range(4)]
+    rows = [mat[k + j : k + j + 1, :] for j in range(4)]
+    d = [[jnp.broadcast_to(mat[k + i : k + i + 1, k + j : k + j + 1], (1, mat.shape[1])) for j in range(i + 1)] for i in range(4)]
+    a00, a01, a11 = inverse_pair(d[0][0], d[1][0], d[1][1])
+    l20, l21 = d[2][0] * a00 + d[2][1] * a01, d[2][0] * a01 + d[2][1] * a11
+    l30, l31 = d[3][0] * a00 + d[3][1] * a01, d[3][0] * a01 + d[3][1] * a11
+    s22 = d[2][2] - (l20 * d[2][0] + l21 * d[2][1])
+    s32 = d[3][2] - (l30 * d[2][0] + l31 * d[2][1])
+    s33 = d[3][3] - (l30 * d[3][0] + l31 * d[3][1])
+    e22, e32, e33 = inverse_pair(s22, s32, s33)
+    e20, e21 = -(e22 * l20 + e32 * l30), -(e22 * l21 + e32 * l31)
+    e30, e31 = -(e32 * l20 + e33 * l30), -(e32 * l21 + e33 * l31)
+    e00 = a00 - (l20 * e20 + l30 * e30)
+    e10 = a01 - (l21 * e20 + l31 * e30)
+    e11 = a11 - (l21 * e21 + l31 * e31)
+    e = [[e00, e10, e20, e30], [e10, e11, e21, e31], [e20, e21, e22, e32], [e30, e31, e32, e33]]
     lane_row = lane[:1]
-    top0 = jnp.where(lane_row == k, -i00, jnp.where(lane_row == k + 1, -i01, top0))
-    top1 = jnp.where(lane_row == k, -i01, jnp.where(lane_row == k + 1, -i11, top1))
-    raw0 = i00 * row0 + i01 * row1
-    raw1 = i01 * row0 + i11 * row1
-    out = mat - col0 * raw0 - col1 * raw1
-    out = jnp.where(lane == k, side0, jnp.where(lane == k + 1, side1, out))
-    out = jnp.where(sub == k, top0, jnp.where(sub == k + 1, top1, out))
-    return out
+    tops = []
+    for i in range(4):
+        top = (e[i][0] * rows[0] + e[i][1] * rows[1]) + (e[i][2] * rows[2] + e[i][3] * rows[3])
+        for j in range(4):
+            top = jnp.where(lane_row == k + j, -e[i][j], top)
+        tops.append(top)
+    out = jnp.where((lane >= k) & (lane < k + 4), 0.0, mat)
+    out = out - ((cols[0] * tops[0] + cols[1] * tops[1]) + (cols[2] * tops[2] + cols[3] * tops[3]))
+    head = out[:SUBLANES]
+    sub = lax.broadcasted_iota(jnp.int32, head.shape, 0)
+    for j in range(4):
+        head = jnp.where(sub == k + j, tops[j], head)
+    return jnp.concatenate([head, out[SUBLANES:]], axis=0)
 
 
 def sweep_groups(mat, count):
     size = mat.shape[0]
     lane = lax.broadcasted_iota(jnp.int32, mat.shape, 1)
-    sub = lax.broadcasted_iota(jnp.int32, mat.shape, 0)
 
     def group(_, mat):
-        for k in range(0, SUBLANES, 2):
-            mat = sweep_pair(mat, k, lane, sub)
+        for k in range(0, SUBLANES, 4):
+            mat = sweep_four(mat, k, lane)
         mat = jnp.concatenate([mat[SUBLANES:], mat[:SUBLANES]], axis=0)
         return pltpu.roll(mat, size - SUBLANES, 1)
 
@@ -96,18 +115,24 @@
     return rows, count
 
 
-def kernel(n, ncols, owner, parent, rhs_t, child_hbm, row_map, col_map, front, panel, coefs, side_t, left_t,
-           child, send, recv, flat, hot, sides, prod, total, halves, gram, gram_in, gram_all,
+def kernel(n, ncols, owner_hbm, parent, rhs_hbm, child_hbm, row_map_hbm, col_map_hbm, front, panel, coefs, side_out,
+           owner, rhs_t, row_map, col_map, child, send, recv, flat, hot, sides, prod, total, halves, gram, gram_in, gram_all,
            in_sem, a2a_send, a2a_recv, pan_send, pan_recv, gram_send, gram_recv, red_send, red_recv):
     row, col = lax.axis_index("rows"), lax.axis_index("cols")
     rows_dev, cols_dev = front.shape
     child_rows, child_cols = child.shape
     nrhs = rhs_t.shape[0]
     block = child_rows // n
-    load_child = pltpu.make_async_copy(child_hbm, child, in_sem.at[0])
-    load_child.start()
-    load = pltpu.make_async_copy(parent, front, in_sem.at[1])
-    load.start()
+    first_loads = [
+        pltpu.make_async_copy(source, target, in_sem.at[k])
+        for k, (source, target) in enumerate([(owner_hbm, owner), (row_map_hbm, row_map), (child_hbm, child)])
+    ]
+    later_loads = [
+        pltpu.make_async_copy(source, target, in_sem.at[3 + k])
+        for k, (source, target) in enumerate([(col_map_hbm, col_map), (rhs_hbm, rhs_t), (parent, front)])
+    ]
+    for load in first_loads + later_loads:
+        load.start()
 
     barrier = pltpu.get_barrier_semaphore()
     for step in range(1, n):
@@ -115,6 +140,8 @@
     for step in range(1, ncols):
         pl.semaphore_signal(barrier, inc=1, device_id=(row, lax.rem(col + step, ncols)), device_id_type=MESH)
 
+    for load in first_loads:
+        load.wait()
     source = lax.broadcasted_iota(jnp.int32, (1, child_rows), 1)
     target = jnp.zeros((1, child_rows), jnp.int32)
     for k in range(n):
@@ -123,7 +150,6 @@
     place_f = jnp.where(place, 1.0, 0.0).astype(f32)
     landing = jnp.sum(place_f * row_map[...].astype(f32), axis=1, keepdims=True)
     place_b = place_f.astype(bf16)
-    load_child.wait()
     one, two, three = pieces(child[...])
     ordered = dot(place_b, one, ((1,), (0,))) + dot(place_b, two, ((1,), (0,))) + dot(place_b, three, ((1,), (0,)))
     landing = jnp.broadcast_to(landing, (child_rows, LANES))
@@ -143,11 +169,12 @@
         copies.append(copy)
     recv[row] = send[row]
 
+    for load in later_loads:
+        load.wait()
     cols_at = lax.broadcasted_iota(jnp.int32, hot.shape, 0)
     hot[...] = jnp.where(cols_at == col_map[...], 1.0, 0.0).astype(f32).astype(bf16)
     padded = jnp.concatenate([rhs_t[...], jnp.zeros((sides.shape[1] - nrhs, rows_dev), f32)], axis=0)
     sides[...] = jnp.transpose(padded)
-    load.wait()
     for copy in copies:
         copy.wait()
 
@@ -332,10 +359,32 @@
             base[q] = marks[stage][q]
 
     inverse = -mat
-    side = dot_full(inverse, total[:, cols_dev:])
+    side_out[...] = dot_full(inverse, total[:, cols_dev:])
     coefs[...] = dot_full(inverse, total[:, :cols_dev])
-    side_t[...] = jnp.transpose(side)[:nrhs]
-    left_t[...] = rhs_t[...] - jnp.transpose(dot_full(panel[...], side))[:nrhs]
+
+
+def finish(front, panel, coefs, side, rhs_t, updated, side_t, left_t, stage, sems):
+    nrhs = rhs_t.shape[0]
+    tile = stage.shape[2]
+    high, low, _ = pieces(panel[...])
+    left = jnp.concatenate([high, high, low], axis=1)
+
+    def product(right):
+        top, rest, _ = pieces(right)
+        return dot(left, jnp.concatenate([top, rest, top], axis=0), ((1,), (0,)))
+
+    copies = []
+    for t in range(stage.shape[0]):
+        at = slice(t * tile, (t + 1) * tile)
+        stage[t] = front[:, at] - product(coefs[:, at])
+        copy = pltpu.make_async_copy(stage.at[t], updated.at[:, pl.ds(t * tile, tile)], sems.at[t])
+        copy.start()
+        copies.append(copy)
+    sides = side[...]
+    side_t[...] = jnp.transpose(sides)[:nrhs]
+    left_t[...] = rhs_t[...] - jnp.transpose(product(sides))[:nrhs]
+    for copy in copies:
+        copy.wait()
 
 
 def solution(mesh):
@@ -353,20 +402,25 @@
         landing_rows, slots = slots_of(n)
         block = child_rows // n
         chunks = min(n, PANEL // SUBLANES)
-        vmem, anywhere = pl.BlockSpec(memory_space=pltpu.VMEM), pl.BlockSpec(memory_space=pl.ANY)
+        vmem = pl.BlockSpec(memory_space=pltpu.VMEM)
         dma = pltpu.SemaphoreType.DMA
-        front, panel, coefs, side_t, left_t = pl.pallas_call(
+        hbm = pl.BlockSpec(memory_space=pltpu.HBM)
+        rhs_t = right_sides.T
+        front, panel, coefs, side = pl.pallas_call(
             functools.partial(kernel, n, ncols),
             out_shape=(
                 jax.ShapeDtypeStruct((rows_dev, cols_dev), f32),
                 jax.ShapeDtypeStruct((rows_dev, PANEL), f32),
                 jax.ShapeDtypeStruct((PANEL, cols_dev), f32),
-                jax.ShapeDtypeStruct((nrhs, PANEL), f32),
-                jax.ShapeDtypeStruct((nrhs, rows_dev), f32),
+                jax.ShapeDtypeStruct((PANEL, side_width), f32),
             ),
-            in_specs=[pl.BlockSpec(memory_space=pltpu.SMEM), anywhere, vmem, anywhere, vmem, vmem],
-            out_specs=(vmem, vmem, vmem, vmem, vmem),
+            in_specs=[hbm] * 6,
+            out_specs=(vmem, vmem, vmem, vmem),
             scratch_shapes=[
+                pltpu.SMEM(block_owner.shape, jnp.int32),
+                pltpu.VMEM((nrhs, rows_dev), f32),
+                pltpu.VMEM((1, child_rows), jnp.int32),
+                pltpu.VMEM((1, child_cols), jnp.int32),
                 pltpu.VMEM((child_rows, child_cols), f32),
                 pltpu.VMEM((n, block, child_cols + LANES), f32),
                 pltpu.VMEM((n, block, child_cols + LANES), f32),
@@ -379,7 +433,7 @@
                 pltpu.VMEM((PANEL, PANEL), f32),
                 pltpu.VMEM((n, PANEL // chunks, PANEL), f32),
                 pltpu.VMEM((PANEL, PANEL), f32),
-                dma((2,)),
+                dma((6,)),
                 dma((n,)),
                 dma((n,)),
                 dma((max(ncols - 1, 1),)),
@@ -390,8 +444,20 @@
                 dma((nparts, 2 * slots)),
             ],
             compiler_params=pltpu.CompilerParams(collective_id=0, has_side_effects=True, vmem_limit_bytes=VMEM_LIMIT),
-        )(block_owner, parent_front, right_sides.T, child_values, row_map.reshape(1, -1), col_map.reshape(1, -1))
-        updated = front - jnp.dot(panel, coefs, precision=lax.Precision.HIGHEST, preferred_element_type=f32)
+        )(block_owner, parent_front, rhs_t, child_values, row_map.reshape(1, -1), col_map.reshape(1, -1))
+        tile = min(TILE, cols_dev)
+        updated, side_t, left_t = pl.pallas_call(
+            finish,
+            out_shape=(
+                jax.ShapeDtypeStruct((rows_dev, cols_dev), f32),
+                jax.ShapeDtypeStruct((nrhs, PANEL), f32),
+                jax.ShapeDtypeStruct((nrhs, rows_dev), f32),
+            ),
+            in_specs=[vmem] * 5,
+            out_specs=(hbm, vmem, vmem),
+            scratch_shapes=[pltpu.VMEM((cols_dev // tile, rows_dev, tile), f32), dma((cols_dev // tile,))],
+            compiler_params=pltpu.CompilerParams(vmem_limit_bytes=16 << 20),
+        )(front, panel, coefs, side, rhs_t)
         return updated, side_t.T, left_t.T
 
     in_specs = (

time: 53.2 us -> 48.1 us (0.904)
  matrix products: 1.98 us -> 0 us
  Pallas kernels: 45.4 us -> 43.6 us
  local copies, waits for them, and re-layouts: 4.87 us -> 3.63 us
    pallas_call x1, Pallas kernels: 45.4 us -> 41.7 us  [shards(): pl.pallas_call(functools.partial(kernel, n, ncols), out_shape=(jax.ShapeD...]
    dot_general x1 -> x0, matrix products: 1.98 us -> none  [shards(): jnp.dot(panel, coefs, precision=lax.Precision.HIGHEST, preferred_element_...]
    pallas_call x0 -> x1, Pallas kernels: none -> 1.9 us  [shards(): pl.pallas_call(finish, out_shape=(jax.ShapeDtypeStruct((rows_dev, cols_de...]
    unnamed x14 -> x12, local copies, waits for them, and re-layouts: 4.87 us -> 3.63 us
where the time goes in v3:
time: 48.1 us; the launch traced here: 47.9 us
  Pallas kernels  43.6 us (91%)
  local copies, waits for them, and re-layouts  3.63 us (8%)
  between operations  0.67 us (1%)
    pallas_call x1, Pallas kernels, shards(): pl.pallas_call(functools.partial(kernel, n, ncols), out_shape=(jax.ShapeD...  41.7 us
    unnamed x12, local copies, waits for them, and re-layouts  3.63 us
    pallas_call x1, Pallas kernels, shards(): pl.pallas_call(finish, out_shape=(jax.ShapeDtypeStruct((rows_dev, cols_de...  1.9 us

profile of v3, /device:TPU:0, one launch (start us, length us, event | category | flops | bytes accessed | tf_op | source)
XLA Modules:
  0.0 47.9 jit_solution(17536229225657842979)
XLA Ops:
  0.6 0.0 copy-start.3
  0.6 0.0 copy-start.4
  0.7 0.0 copy-start.5
  0.7 0.7 %copy-done.3 = s32[512]{0:T(512)S(1)} copy-done((s32[512]{0:T(512)S(1)}, s32[512]{0:T(512)}, u32[]{:S(2)}) %copy-start.3) | copy-done | bytes 2072
  1.3 0.0 copy-done.4
  1.3 0.0 copy-done.5
  1.3 0.0 copy-start
  1.3 1.2 %copy-done = f32[256,1024]{1,0:T(8,128)S(1)} copy-done((f32[256,1024]{1,0:T(8,128)S(1)}, f32[256,1024]{1,0:T(8,128)}, u32[]{:S(2)}) %copy-start) | copy-done | bytes 1048600
  2.5 0.0 copy-start.1
  2.5 0.8 %copy-done.1 = f32[256,64]{0,1:T(8,128)S(1)} copy-done((f32[256,64]{0,1:T(8,128)S(1)}, f32[256,64]{0,1:T(8,128)}, u32[]{:S(2)}) %copy-start.1) | copy-done | bytes 65560
  3.4 0.0 copy-start.2
  3.4 0.9 %copy-done.2 = f32[64,512]{1,0:T(8,128)S(1)} copy-done((f32[64,512]{1,0:T(8,128)S(1)}, f32[64,512]{1,0:T(8,128)}, u32[]{:S(2)}) %copy-start.2) | copy-done | bytes 131096
  4.3 41.7 %shard_map.85 = (f32[256,1024]{1,0:T(8,128)S(1)}, f32[256,128]{1,0:T(8,128)S(1)}, f32[128,1024]{1,0:T(8,128)S(1)}, f32[128,128]{1,0:T(8,128)S(1)}) custom-call(s32[16]{0:T(128)S(1)} %copy-done.4, f32[256,1024]{1,0:T(8,128)S(1)} %copy-done, f32[64,256]{1,0:T(8,128)S(1)} %bitcast.5, f32[64,512]{1,0:T(8,128)S(1)} %copy-done.2, s32[1,64]{1,0:T(1,128)S(1)} %bitcast.8, ...), custom_call_target="tpu_custom_call" | custom-call | tf_op jit(solution)/shard_map/pallas_call | solution.py:409
  46.0 1.9 %shard_map.86 = (f32[256,1024]{1,0:T(8,128)}, f32[64,128]{1,0:T(8,128)}, f32[64,256]{1,0:T(8,128)}) custom-call(f32[256,1024]{1,0:T(8,128)S(1)} %get-tuple-element.10.front, f32[256,128]{1,0:T(8,128)S(1)} %get-tuple-element.11.panel, f32[128,1024]{1,0:T(8,128)S(1)} %get-tuple-element.12.coefs, f32[128,128]{1,0:T(8,128)S(1)} %get-tuple-element.13.side, ...), custom_call_target="tpu_custom_call" | custom-call | tf_op jit(solution)/shard_map/pallas_call | solution.py:449
Async XLA Ops:
  0.6 0.7 %copy-start.3 = (s32[512]{0:T(512)S(1)}, s32[512]{0:T(512)}, u32[]{:S(2)}) copy-start(s32[512]{0:T(512)} %param.11) | copy-start | bytes 6148
  0.6 0.7 %copy-start.4 = (s32[16]{0:T(128)S(1)}, s32[16]{0:T(128)}, u32[]{:S(2)}) copy-start(s32[16]{0:T(128)} %owner_hbm.1) | copy-start | bytes 196
  0.7 0.7 %copy-start.5 = (s32[64]{0:T(128)S(1)}, s32[64]{0:T(128)}, u32[]{:S(2)}) copy-start(s32[64]{0:T(128)} %param.10) | copy-start | bytes 772
  1.3 1.2 %copy-start = (f32[256,1024]{1,0:T(8,128)S(1)}, f32[256,1024]{1,0:T(8,128)}, u32[]{:S(2)}) copy-start(f32[256,1024]{1,0:T(8,128)} %parent.1) | copy-start | bytes 3145732
  2.5 0.8 %copy-start.1 = (f32[256,64]{0,1:T(8,128)S(1)}, f32[256,64]{0,1:T(8,128)}, u32[]{:S(2)}) copy-start(f32[256,64]{0,1:T(8,128)} %param.7) | copy-start | bytes 196612
  3.4 0.9 %copy-start.2 = (f32[64,512]{1,0:T(8,128)S(1)}, f32[64,512]{1,0:T(8,128)}, u32[]{:S(2)}) copy-start(f32[64,512]{1,0:T(8,128)} %child_hbm.1) | copy-start | bytes 393220

commit v4 on v3

--- a/solution.py
+++ b/solution.py
@@ -11,7 +11,7 @@
 LANES = 128
 SUBLANES = 8
 TILE = 256
-VMEM_LIMIT = 40 << 20
+VMEM_LIMIT = 67043328
 MESH = pl.DeviceIdType.MESH
 f32 = jnp.float32
 bf16 = jnp.bfloat16
@@ -115,8 +115,8 @@
     return rows, count
 
 
-def kernel(n, ncols, owner_hbm, parent, rhs_hbm, child_hbm, row_map_hbm, col_map_hbm, front, panel, coefs, side_out,
-           owner, rhs_t, row_map, col_map, child, send, recv, flat, hot, sides, prod, total, halves, gram, gram_in, gram_all,
+def kernel(n, ncols, owner_hbm, parent, rhs_hbm, child_hbm, row_map_hbm, col_map_hbm,
+           front_out, panel_out, coefs_out, side_out, front, panel, coefs, side, out_sem, owner, rhs_t, row_map, col_map, child, send, recv, flat, hot, sides, prod, total, halves, gram, gram_in, gram_all,
            in_sem, a2a_send, a2a_recv, pan_send, pan_recv, gram_send, gram_recv, red_send, red_recv):
     row, col = lax.axis_index("rows"), lax.axis_index("cols")
     rows_dev, cols_dev = front.shape
@@ -237,8 +237,19 @@
         gathers.append(copy)
     gram_in[row] = gram[own_rows, :]
 
-    prod[:, :cols_dev] = dot_full(block_panel, front[...], trans)
-    prod[:, cols_dev:] = dot_full(block_panel, sides[...], trans)
+    def products(first, last):
+        split = min(max(first, cols_dev), last)
+        if split > first:
+            prod[:, first:split] = dot_full(block_panel, front[:, first:split], trans)
+        if last > split:
+            prod[:, split:last] = dot_full(block_panel, sides[:, split - cols_dev : last - cols_dev], trans)
+
+    keep_copies = [
+        pltpu.make_async_copy(front, front_out, out_sem.at[0]),
+        pltpu.make_async_copy(panel, panel_out, out_sem.at[1]),
+    ]
+    for copy in keep_copies:
+        copy.start()
 
     starts, parts, halving = plan(n, prod.shape[1])
     base = [row * 0] * len(parts)
@@ -260,31 +271,39 @@
             others.append((code, peer))
         return mine, others
 
-    def send_stage(stage, at, slot, size, split):
+    def send_part(q, stage, at, slot, size, split):
+        groups, extras = parts[q]
+        bits = groups[stage] if split else extras[stage]
+        mine, others = members(bits)
+        piece = size >> len(bits) if split else size
+        keep = pl.multiple_of(base[q] + mine * piece if split else base[q], SUBLANES)
+        width = starts[q + 1] - starts[q]
+        sent = []
+        for d, (code, peer) in enumerate(others):
+            give = pl.multiple_of(base[q] + code * piece, SUBLANES) if split else keep
+            copy = pltpu.make_async_remote_copy(
+                src_ref=prod.at[pl.ds(give, piece), pl.ds(starts[q], width)],
+                dst_ref=halves.at[q, pl.ds(at + d * piece, piece), pl.ds(0, width)],
+                send_sem=red_send.at[q, slot + d], recv_sem=red_recv.at[q, slot + d],
+                device_id=(peer, col), device_id_type=MESH)
+            copy.start()
+            sent.append((copy, at + d * piece))
+        base[q] = keep
+        return sent, keep, piece, width
+
+    def send_stage(stage, at, slot, size, split, before):
         held = []
-        for q, (groups, extras) in enumerate(parts):
-            bits = groups[stage] if split else extras[stage]
-            mine, others = members(bits)
-            piece = size >> len(bits) if split else size
-            keep = pl.multiple_of(base[q] + mine * piece if split else base[q], SUBLANES)
-            width = starts[q + 1] - starts[q]
-            sent = []
-            for d, (code, peer) in enumerate(others):
-                give = pl.multiple_of(base[q] + code * piece, SUBLANES) if split else keep
-                copy = pltpu.make_async_remote_copy(
-                    src_ref=prod.at[pl.ds(give, piece), pl.ds(starts[q], width)],
-                    dst_ref=halves.at[q, pl.ds(at + d * piece, piece), pl.ds(0, width)],
-                    send_sem=red_send.at[q, slot + d], recv_sem=red_recv.at[q, slot + d],
-                    device_id=(peer, col), device_id_type=MESH)
-                copy.start()
-                sent.append((copy, at + d * piece))
-            held.append((sent, keep, piece, width))
-            base[q] = keep
-        used = len(held[0][0])
-        return held, at + used * held[0][2], slot + used, held[0][2]
-
-    def add_stage(held):
-        for q, (sent, keep, piece, width) in enumerate(held):
+        for q in range(len(parts)):
+            before(q)
+            if split:
+                marks[q].append(base[q])
+            held.append(send_part(q, stage, at, slot, size, split))
+        used, piece = len(held[0][0]), held[0][2]
+        return held, at + used * piece, slot + used, piece
+
+    def adder(held):
+        def add_part(q):
+            sent, keep, piece, width = held[q]
             for copy, _ in sent:
                 copy.wait()
             spot = (pl.ds(keep, piece), slice(starts[q], starts[q + 1]))
@@ -293,24 +312,24 @@
                 value = value + halves[q, at : at + piece, :width]
             prod[spot] = value
 
-    def share_stage(stage, slot, piece):
+        return add_part
+
+    def share_part(q, stage, slot, piece):
+        _, others = members(parts[q][0][stage])
+        keep = pl.multiple_of(base[q], SUBLANES)
+        spot = total.at[pl.ds(keep, piece), pl.ds(starts[q], starts[q + 1] - starts[q])]
         sent = []
-        for q, (groups, _) in enumerate(parts):
-            _, others = members(groups[stage])
-            keep = pl.multiple_of(base[q], SUBLANES)
-            spot = total.at[pl.ds(keep, piece), pl.ds(starts[q], starts[q + 1] - starts[q])]
-            for d, (_, peer) in enumerate(others):
-                copy = pltpu.make_async_remote_copy(
-                    src_ref=spot, dst_ref=spot, send_sem=red_send.at[q, slot + d], recv_sem=red_recv.at[q, slot + d],
-                    device_id=(peer, col), device_id_type=MESH)
-                copy.start()
-                sent.append(copy)
-        return sent, slot + len(sent) // len(parts)
-
-    marks = []
+        for d, (_, peer) in enumerate(others):
+            copy = pltpu.make_async_remote_copy(
+                src_ref=spot, dst_ref=spot, send_sem=red_send.at[q, slot + d], recv_sem=red_recv.at[q, slot + d],
+                device_id=(peer, col), device_id_type=MESH)
+            copy.start()
+            sent.append(copy)
+        return sent
+
+    marks = [[] for _ in parts]
     at, slot, size = 0, 0, PANEL
-    marks.append(list(base))
-    held, at, slot, size = send_stage(0, at, slot, size, True)
+    held, at, slot, size = send_stage(0, at, slot, size, True, lambda q: products(starts[q], starts[q + 1]))
 
     for copy in gathers:
         copy.wait()
@@ -329,9 +348,7 @@
         spreads.append(copy)
 
     for stage in range(1, nstages):
-        add_stage(held)
-        marks.append(list(base))
-        held, at, slot, size = send_stage(stage, at, slot, size, True)
+        held, at, slot, size = send_stage(stage, at, slot, size, True, adder(held))
     for copy in spreads:
         copy.wait()
     turns = PANEL // SUBLANES
@@ -342,30 +359,57 @@
         return (sweep_groups(mat, upto - done) if upto > done else mat), upto
 
     mat, done = turn_by(mat, done, 3)
-    add_stage(held)
     for stage in range(len(parts[0][1])):
-        held, at, slot, size = send_stage(stage, at, slot, size, False)
-        add_stage(held)
+        held, at, slot, size = send_stage(stage, at, slot, size, False, adder(held))
+    last_add = adder(held)
+    waiting = [[] for _ in parts]
+    for stage in reversed(range(nstages)):
+        for q in range(len(parts)):
+            if stage == nstages - 1:
+                last_add(q)
+                spot = (pl.ds(pl.multiple_of(base[q], SUBLANES), size), slice(starts[q], starts[q + 1]))
+                total[spot] = prod[spot]
+            for copy in waiting[q]:
+                copy.wait()
+            waiting[q] = share_part(q, stage, slot, size)
+            base[q] = marks[q][stage]
+        slot += len(waiting[0])
+        mat, done = turn_by(mat, done, turns if stage == 0 else 4)
+        size <<= len(parts[0][0][stage])
+
+    inverse = -mat
     for q in range(len(parts)):
-        spot = (pl.ds(pl.multiple_of(base[q], SUBLANES), size), slice(starts[q], starts[q + 1]))
-        total[spot] = prod[spot]
-    for stage in reversed(range(nstages)):
-        sent, slot = share_stage(stage, slot, size)
-        mat, done = turn_by(mat, done, turns if stage == 0 else 4)
-        for copy in sent:
+        for copy in waiting[q]:
             copy.wait()
-        size <<= len(parts[0][0][stage])
-        for q in range(len(parts)):
-            base[q] = marks[stage][q]
-
-    inverse = -mat
-    side_out[...] = dot_full(inverse, total[:, cols_dev:])
-    coefs[...] = dot_full(inverse, total[:, :cols_dev])
-
-
-def finish(front, panel, coefs, side, rhs_t, updated, side_t, left_t, stage, sems):
+        first, last = starts[q], starts[q + 1]
+        split = min(max(first, cols_dev), last)
+        if split > first:
+            coefs[:, first:split] = dot_full(inverse, total[:, first:split])
+            copy = pltpu.make_async_copy(
+                coefs.at[:, pl.ds(first, split - first)], coefs_out.at[:, pl.ds(first, split - first)], out_sem.at[2 + q])
+            copy.start()
+            keep_copies.append(copy)
+        if last > split:
+            side[:, split - cols_dev : last - cols_dev] = dot_full(inverse, total[:, split:last])
+    copy = pltpu.make_async_copy(side, side_out, out_sem.at[2 + len(parts)])
+    copy.start()
+    keep_copies.append(copy)
+    for copy in keep_copies:
+        copy.wait()
+
+
+def finish(front_hbm, panel_hbm, coefs_hbm, side_hbm, rhs_hbm, updated, side_t, left_t,
+           front, panel, coefs, side, rhs_t, stage, in_sem, sems):
     nrhs = rhs_t.shape[0]
     tile = stage.shape[2]
+    loads = [
+        pltpu.make_async_copy(source, target, in_sem.at[k])
+        for k, (source, target) in enumerate(
+            [(panel_hbm, panel), (coefs_hbm, coefs), (front_hbm, front), (side_hbm, side), (rhs_hbm, rhs_t)])
+    ]
+    for load in loads:
+        load.start()
+    loads[0].wait()
     high, low, _ = pieces(panel[...])
     left = jnp.concatenate([high, high, low], axis=1)
 
@@ -373,6 +417,8 @@
         top, rest, _ = pieces(right)
         return dot(left, jnp.concatenate([top, rest, top], axis=0), ((1,), (0,)))
 
+    for load in loads[1:]:
+        load.wait()
     copies = []
     for t in range(stage.shape[0]):
         at = slice(t * tile, (t + 1) * tile)
@@ -415,8 +461,13 @@
                 jax.ShapeDtypeStruct((PANEL, side_width), f32),
             ),
             in_specs=[hbm] * 6,
-            out_specs=(vmem, vmem, vmem, vmem),
+            out_specs=(hbm, hbm, hbm, hbm),
             scratch_shapes=[
+                pltpu.VMEM((rows_dev, cols_dev), f32),
+                pltpu.VMEM((rows_dev, PANEL), f32),
+                pltpu.VMEM((PANEL, cols_dev), f32),
+                pltpu.VMEM((PANEL, side_width), f32),
+                dma((3 + nparts,)),
                 pltpu.SMEM(block_owner.shape, jnp.int32),
                 pltpu.VMEM((nrhs, rows_dev), f32),
                 pltpu.VMEM((1, child_rows), jnp.int32),
@@ -453,10 +504,19 @@
                 jax.ShapeDtypeStruct((nrhs, PANEL), f32),
                 jax.ShapeDtypeStruct((nrhs, rows_dev), f32),
             ),
-            in_specs=[vmem] * 5,
+            in_specs=[hbm] * 5,
             out_specs=(hbm, vmem, vmem),
-            scratch_shapes=[pltpu.VMEM((cols_dev // tile, rows_dev, tile), f32), dma((cols_dev // tile,))],
-            compiler_params=pltpu.CompilerParams(vmem_limit_bytes=16 << 20),
+            scratch_shapes=[
+                pltpu.VMEM((rows_dev, cols_dev), f32),
+                pltpu.VMEM((rows_dev, PANEL), f32),
+                pltpu.VMEM((PANEL, cols_dev), f32),
+                pltpu.VMEM((PANEL, side_width), f32),
+                pltpu.VMEM((nrhs, rows_dev), f32),
+                pltpu.VMEM((cols_dev // tile, rows_dev, tile), f32),
+                dma((5,)),
+                dma((cols_dev // tile,)),
+            ],
+            compiler_params=pltpu.CompilerParams(vmem_limit_bytes=VMEM_LIMIT),
         )(front, panel, coefs, side, rhs_t)
         return updated, side_t.T, left_t.T
 

time: 48.1 us -> 44.9 us (0.933)
  local copies, waits for them, and re-layouts: 3.63 us -> 0 us
  Pallas kernels: 43.6 us -> 44.1 us
    unnamed x12 -> x0, local copies, waits for them, and re-layouts: 3.63 us -> none
    pallas_call x1, Pallas kernels: 1.9 us -> 3.41 us  [shards(): pl.pallas_call(finish, out_shape=(jax.ShapeDtypeStruct((rows_dev, cols_de...]
    pallas_call x1, Pallas kernels: 41.7 us -> 40.7 us  [shards(): pl.pallas_call(functools.partial(kernel, n, ncols), out_shape=(jax.ShapeD...]
where the time goes in v4:
time: 44.9 us; the launch traced here: 44.7 us
  Pallas kernels  44.1 us (98%)
  between operations  0.64 us (1%)
    pallas_call x1, Pallas kernels, shards(): pl.pallas_call(functools.partial(kernel, n, ncols), out_shape=(jax.ShapeD...  40.7 us
    pallas_call x1, Pallas kernels, shards(): pl.pallas_call(finish, out_shape=(jax.ShapeDtypeStruct((rows_dev, cols_de...  3.41 us

profile of v4, /device:TPU:0, one launch (start us, length us, event | category | flops | bytes accessed | tf_op | source)
XLA Modules:
  0.0 44.7 jit_solution(11981633726490267417)
XLA Ops:
  0.6 40.7 %shard_map.85 = (f32[256,1024]{1,0:T(8,128)}, f32[256,128]{1,0:T(8,128)}, f32[128,1024]{1,0:T(8,128)}, f32[128,128]{1,0:T(8,128)}) custom-call(s32[16]{0:T(128)} %owner_hbm.1, f32[256,1024]{1,0:T(8,128)} %parent.1, f32[64,256]{1,0:T(8,128)} %bitcast.5, f32[64,512]{1,0:T(8,128)} %child_hbm.1, s32[1,64]{1,0:T(1,128)} %bitcast.8, s32[1,512]{1,0:T(1,128)} %bitcast.7), custom_call_target="tpu_custom_call" | custom-call | tf_op jit(solution)/shard_map/pallas_call | solution.py:455
  41.3 3.4 %shard_map.86 = (f32[256,1024]{1,0:T(8,128)}, f32[64,128]{1,0:T(8,128)}, f32[64,256]{1,0:T(8,128)}) custom-call(f32[256,1024]{1,0:T(8,128)} %get-tuple-element.10.front_hbm, f32[256,128]{1,0:T(8,128)} %get-tuple-element.11.panel_hbm, f32[128,1024]{1,0:T(8,128)} %get-tuple-element.12.coefs_hbm, f32[128,128]{1,0:T(8,128)} %get-tuple-element.13.side_hbm, ...), custom_call_target="tpu_custom_call" | custom-call | tf_op jit(solution)/shard_map/pallas_call | solution.py:500
